TPU v7x, 32 devices: a whole 2x2x4 slice. The times are simulated.
32 devices in a mesh: pipe: 4 (over z), ctx: 8 (over y, x, core).
Axes of the slice: x: 2, y: 2, z: 4, core: 2. Of those that a mesh axis runs over, the one named last changes fastest.
Arguments:
- queries: bfloat16 [4, 2048, 2048], P('pipe', 'ctx'), may hold values from -120 to 120
- keys: bfloat16 [4, 2048, 512], P('pipe', 'ctx'), may hold values from -6.5 to 6.5
- values: bfloat16 [4, 2048, 512], P('pipe', 'ctx'), may hold values from -24 to 24
- out_weight: bfloat16 [4, 2048, 4096], P('pipe'), may hold values from -0.125 to 0.125
Outputs:
- handed: bfloat16 [4, 2048, 4096], P('pipe', 'ctx')
All inputs are finite; a program needn't handle non-finite values.
Results may differ from a plain program's by a relative error of at most 0.0065.
Values may be sent and summed in bfloat16 or wider, within the bound.
A program may use at most 128 MiB of HBM per device.

v0:
```python
import functools
import math

import jax
import jax.numpy as jnp
from jax import lax
from jax.experimental import pallas as pl
from jax.experimental.pallas import tpu as pltpu
from jax.sharding import PartitionSpec as P

HEAD_SIZE = 128
COLUMNS = 256
MOVED = 2
EXTRA = 16
VMEM_LIMIT = 50 * 1024 * 1024
MESH = pl.DeviceIdType.MESH


def kernel(sections, spans, across, q_ref, k_ref, v_ref, w_ref, o_ref, held, weight, stacked, acc, top,
           attended, projected, pair_send, far_send, pass_send, relay_send, span_recv, weight_sem, out_send, out_recv, own_sem, query_sem,
           aside, landed, aside_recv, cross_send, cross_recv, final_send):
    rows, kv_width = k_ref.shape
    q_width = q_ref.shape[1]
    heads = kv_width // HEAD_SIZE
    group = q_width // kv_width
    chips = spans // 2
    pieces = weight.shape[0]
    section = lax.axis_index("pipe")
    me = lax.axis_index("ctx")
    chip, core = me // 2, lax.rem(me, 2)
    line, column = chip // across, lax.rem(chip, across)
    lines = chips // across
    following = lax.rem(section + 1, sections)
    before = lax.rem(section + sections - 1, sections)
    factor = math.log2(math.e) / math.sqrt(HEAD_SIZE)

    barrier = pltpu.get_barrier_semaphore()

    @pl.loop(1, spans)
    def _(step):
        pl.semaphore_signal(barrier, inc=1, device_id={"ctx": lax.rem(me + step, spans)}, device_id_type=MESH)

    for neighbour in (before, following):
        pl.semaphore_signal(barrier, inc=1, device_id={"pipe": neighbour}, device_id_type=MESH)

    def weight_copy(piece):
        return pltpu.make_async_copy(
            w_ref.at[:, pl.ds(pl.multiple_of(piece * COLUMNS, COLUMNS), COLUMNS)],
            weight.at[piece], weight_sem.at[piece])

    def place(owner, side, which):
        return held.at[owner, which, pl.ds(pl.multiple_of(side * rows, rows), rows), :]

    def own_copy(which):
        return pltpu.make_async_copy((k_ref, v_ref)[which], place(chip, core, which), own_sem.at[which])

    def query_copy(head, member):
        at = head * group + member
        return pltpu.make_async_copy(
            q_ref.at[:, at * HEAD_SIZE:(at + 1) * HEAD_SIZE],
            stacked.at[head, member * rows:(member + 1) * rows, :], query_sem.at[at])

    for which in range(2):
        own_copy(which).start()
    for head in range(heads):
        for member in range(group):
            query_copy(head, member).start()

    @pl.loop(0, pieces)
    def _(piece):
        weight_copy(piece).start()

    for which in range(2):
        own_copy(which).wait()

    def pair_copy(which):
        return pltpu.make_async_remote_copy(
            place(chip, core, which), place(chip, core, which), pair_send.at[which],
            span_recv.at[chip, core, which], device_id={"ctx": chip * 2 + 1 - core}, device_id_type=MESH)

    def far_copy(target, which):
        return pltpu.make_async_remote_copy(
            place(chip, core, which), place(chip, core, which), far_send.at[target, which],
            span_recv.at[chip, core, which], device_id={"ctx": target * 2 + core}, device_id_type=MESH)

    def pass_copy(owner, which):
        return pltpu.make_async_remote_copy(
            place(owner, core, which), place(owner, core, which), pass_send.at[owner, which],
            span_recv.at[owner, core, which], device_id={"ctx": chip * 2 + 1 - core}, device_id_type=MESH)

    def relay_copy(owner, target, which):
        return pltpu.make_async_remote_copy(
            place(owner, core, which), place(owner, core, which), relay_send.at[owner, target],
            span_recv.at[owner, core, which], device_id={"ctx": target * 2 + core}, device_id_type=MESH)

    def each_own(act):
        @pl.loop(1, across)
        def _(step):
            other = lax.rem(column + step, across)

            @pl.when((line < lines - 1) | (other > column))
            def _():
                act(line * across + other, 0)

        @pl.loop(line + 1, lines)
        def _(other):
            act(other * across + column, 1)
            act(other * across + column, 0)

        @pl.loop(column + 1, across)
        def _(other):
            act(line * across + other, 1)

    def each_key_source(act):
        @pl.when(line < lines - 1)
        def _():
            @pl.loop(1, across)
            def _(step):
                act(line * across + lax.rem(column + step, across))

    def each_key_relay(owner, act):
        @pl.loop(line + 1, lines)
        def _(other):
            act(owner, other * across + column, 0)

    def each_value_source(act):
        @pl.loop(0, line)
        def _(other):
            act(other * across + column)

    def each_value_relay(owner, act):
        @pl.loop(1, across)
        def _(step):
            act(owner, line * across + lax.rem(column + step, across), 1)

    def wait_span(owner, side, which):
        pltpu.make_async_remote_copy(
            place(owner, side, which), place(owner, side, which), pair_send.at[which],
            span_recv.at[owner, side, which], device_id={"ctx": chip * 2 + 1 - core}, device_id_type=MESH).wait_recv()

    pl.semaphore_wait(barrier, spans + 1)
    for which in range(2):
        pair_copy(which).start()

    each_own(lambda target, which: far_copy(target, which).start())

    for head in range(heads):
        for member in range(group):
            query_copy(head, member).wait()

    def block(owner, head, first):
        lanes = slice(head * HEAD_SIZE, (head + 1) * HEAD_SIZE)
        scores = lax.dot_general(
            held[owner, 0, :, lanes], stacked[head], (((1,), (1,)), ((), ())),
            preferred_element_type=jnp.float32)
        if first:
            key = lax.broadcasted_iota(jnp.int32, scores.shape, 0)
            row = lax.rem(lax.broadcasted_iota(jnp.int32, scores.shape, 1), rows) + core * rows
            scores = jnp.where(key <= row, scores, -1e30)
        highest = jnp.max(scores, axis=0, keepdims=True)
        if not first:
            previous = top[head]
            highest = jnp.maximum(previous, highest)
            rescale = jnp.exp2((previous - highest) * factor)
        top[head] = highest
        weights = jnp.exp2((scores - highest) * factor).astype(jnp.bfloat16)
        values = held[owner, 1, :, lanes].T
        values = jnp.concatenate([values, jnp.ones((EXTRA, values.shape[1]), values.dtype)], axis=0)
        summed = jnp.dot(values, weights, preferred_element_type=jnp.float32)
        if first:
            acc[head] = summed
        else:
            acc[head] = acc[head] * rescale + summed

    for which in range(2):
        wait_span(chip, 1 - core, which)

    for head in range(heads):
        block(chip, head, True)

    def relay_keys(owner):
        wait_span(owner, core, 0)
        each_key_relay(owner, lambda *at: relay_copy(*at).start())

        @pl.when(owner < chip)
        def _():
            pass_copy(owner, 0).start()

    def relay_values(owner):
        wait_span(owner, core, 1)
        each_value_relay(owner, lambda *at: relay_copy(*at).start())
        pass_copy(owner, 1).start()

    each_value_source(relay_values)
    each_key_source(relay_keys)

    @pl.loop(0, chip)
    def _(step):
        owner = chip - 1 - step

        @pl.when((owner // across != line) | (line == lines - 1))
        def _():
            wait_span(owner, core, 0)
            pass_copy(owner, 0).start()

        @pl.when((lax.rem(owner, across) != column) | (owner // across == line))
        def _():
            wait_span(owner, core, 1)
            pass_copy(owner, 1).start()

        for which in range(2):
            wait_span(owner, 1 - core, which)

        for head in range(heads):
            block(owner, head, False)

    for head in range(heads):
        for member in range(group):
            part = acc[head, :, member * rows:(member + 1) * rows]
            attended[:, (head * group + member) * HEAD_SIZE:(head * group + member + 1) * HEAD_SIZE] = (
                part[:HEAD_SIZE] / part[HEAD_SIZE:HEAD_SIZE + 1]).T.astype(jnp.bfloat16)

    def out_copy(piece):
        return pltpu.make_async_remote_copy(
            projected.at[piece],
            o_ref.at[:, pl.ds(pl.multiple_of(piece * COLUMNS, COLUMNS), COLUMNS)],
            out_send.at[piece], out_recv.at[piece], device_id={"pipe": following}, device_id_type=MESH)

    late = chips - chips // 2
    heavy = chip >= late
    slot_of = lax.rem(chip + 2 * chips - late, 2)

    def aside_copy(piece):
        return pltpu.make_async_remote_copy(
            projected.at[piece], aside.at[slot_of, piece], out_send.at[piece],
            aside_recv.at[slot_of, piece],
            device_id={"ctx": (chip - late) // 2 * 2 + core}, device_id_type=MESH)

    def cross_copy(slot, piece):
        return pltpu.make_async_remote_copy(
            aside.at[slot, piece], landed.at[slot, piece], cross_send.at[slot, piece],
            cross_recv.at[slot, piece], device_id={"pipe": following}, device_id_type=MESH)

    def final_copy(slot, piece):
        return pltpu.make_async_remote_copy(
            landed.at[slot, piece],
            o_ref.at[:, pl.ds(pl.multiple_of(piece * COLUMNS, COLUMNS), COLUMNS)],
            final_send.at[slot, piece], out_recv.at[piece],
            device_id={"ctx": (late + chip * 2 + slot) * 2 + core}, device_id_type=MESH)

    def each_carried(act):
        @pl.loop(0, jnp.clip(chips // 2 - chip * 2, 0, 2))
        def _(slot):
            @pl.loop(0, MOVED)
            def _(piece):
                act(slot, piece)

    def carry(slot, piece):
        pltpu.make_async_remote_copy(
            aside.at[slot, piece], aside.at[slot, piece], cross_send.at[slot, piece],
            aside_recv.at[slot, piece], device_id={"pipe": following}, device_id_type=MESH).wait_recv()
        cross_copy(slot, piece).start()

    def deliver(slot, piece):
        cross_copy(slot, piece).wait_recv()
        final_copy(slot, piece).start()

    def settle(slot, piece):
        cross_copy(slot, piece).wait_send()
        final_copy(slot, piece).wait_send()

    @pl.loop(0, pieces)
    def _(piece):
        weight_copy(piece).wait()
        projected[piece] = jnp.dot(
            attended[...], weight[piece], preferred_element_type=jnp.float32).astype(jnp.bfloat16)

        @pl.when(heavy & (piece < MOVED))
        def _():
            aside_copy(piece).start()

        @pl.when(jnp.logical_not(heavy & (piece < MOVED)))
        def _():
            out_copy(piece).start()

    each_carried(carry)
    each_carried(deliver)

    for which in range(2):
        pair_copy(which).wait_send()

    each_own(lambda target, which: far_copy(target, which).wait_send())
    each_key_source(lambda owner: each_key_relay(
        owner, lambda *at: relay_copy(*at).wait_send()))
    each_value_source(lambda owner: each_value_relay(
        owner, lambda *at: relay_copy(*at).wait_send()))

    @pl.loop(0, chip)
    def _(owner):
        for which in range(2):
            pass_copy(owner, which).wait_send()

    each_carried(settle)

    @pl.loop(0, pieces)
    def _(piece):
        out_copy(piece).wait()


def per_device(sections, spans, queries, keys, values, out_weight):
    rows, q_width = queries.shape[1:]
    kv_width = keys.shape[2]
    width = out_weight.shape[2]
    heads = kv_width // HEAD_SIZE
    stack = q_width // kv_width * rows
    pieces = width // COLUMNS
    chips = spans // 2
    across = math.isqrt(chips)
    across = across if chips % across == 0 else chips
    hbm = pl.BlockSpec(memory_space=pltpu.HBM)
    handed = pl.pallas_call(
        functools.partial(kernel, sections, spans, across),
        out_shape=jax.ShapeDtypeStruct((rows, width), jnp.bfloat16),
        in_specs=[hbm] * 4,
        out_specs=pl.BlockSpec(memory_space=pl.ANY),
        scratch_shapes=[
            pltpu.VMEM((chips, 2, 2 * rows, kv_width), jnp.bfloat16),
            pltpu.VMEM((pieces, q_width, COLUMNS), jnp.bfloat16),
            pltpu.VMEM((heads, stack, HEAD_SIZE), jnp.bfloat16),
            pltpu.VMEM((heads, HEAD_SIZE + EXTRA, stack), jnp.float32),
            pltpu.VMEM((heads, 1, stack), jnp.float32),
            pltpu.VMEM((rows, q_width), jnp.bfloat16),
            pltpu.VMEM((pieces, rows, COLUMNS), jnp.bfloat16),
            pltpu.SemaphoreType.DMA((2,)),
            pltpu.SemaphoreType.DMA((chips, 2)),
            pltpu.SemaphoreType.DMA((chips, 2)),
            pltpu.SemaphoreType.DMA((chips, chips)),
            pltpu.SemaphoreType.DMA((chips, 2, 2)),
            pltpu.SemaphoreType.DMA((pieces,)),
            pltpu.SemaphoreType.DMA((pieces,)),
            pltpu.SemaphoreType.DMA((pieces,)),
            pltpu.SemaphoreType.DMA((2,)),
            pltpu.SemaphoreType.DMA((q_width // HEAD_SIZE,)),
            pltpu.VMEM((2, MOVED, rows, COLUMNS), jnp.bfloat16),
            pltpu.VMEM((2, MOVED, rows, COLUMNS), jnp.bfloat16),
            pltpu.SemaphoreType.DMA((2, MOVED)),
            pltpu.SemaphoreType.DMA((2, MOVED)),
            pltpu.SemaphoreType.DMA((2, MOVED)),
            pltpu.SemaphoreType.DMA((2, MOVED)),
        ],
        compiler_params=pltpu.CompilerParams(
            collective_id=0, has_side_effects=True, vmem_limit_bytes=VMEM_LIMIT),
    )(*(pltpu.with_memory_space_constraint(each[0], pltpu.HBM) for each in (queries, keys, values, out_weight)))
    return handed[None]


def solution(mesh):
    placed = (
        P("pipe", "ctx", None),
        P("pipe", "ctx", None),
        P("pipe", "ctx", None),
        P("pipe", None, None),
    )
    return jax.shard_map(
        functools.partial(per_device, mesh.shape["pipe"], mesh.shape["ctx"]),
        mesh=mesh, in_specs=placed, out_specs=P("pipe", "ctx", None), check_vma=False
    )
```

profile of v0, /device:TPU:4, one launch (start us, length us, event | category | flops | bytes accessed | tf_op | source)
XLA Modules:
  0.0 78.4 jit_solution(8269223570041048284)
XLA Ops:
  0.0 77.1 %shard_map.46 = bf16[256,4096]{1,0:T(8,128)(2,1)S(1)} custom-call(bf16[256,2048]{1,0:T(8,128)(2,1)} %bitcast.7, bf16[256,512]{1,0:T(8,128)(2,1)} %bitcast.8, bf16[256,512]{1,0:T(8,128)(2,1)} %bitcast.9, bf16[2048,4096]{1,0:T(8,128)(2,1)} %bitcast.6), custom_call_target="tpu_custom_call" | custom-call | tf_op jit(solution)/shard_map/pallas_call | solution.py:321
  77.1 1.3 %copy.6 = bf16[1,256,4096]{2,1,0:T(8,128)(2,1)} copy(bf16[1,256,4096]{2,1,0:T(8,128)(2,1)S(1)} %bitcast.5) | data formatting | bytes 4194304
where the time goes:
time: 78.6 us; the launch traced here: 78.4 us
  Pallas kernels  77.1 us (98%)
  local copies, waits for them, and re-layouts  1.32 us (2%)
    pallas_call x1, Pallas kernels, per_device(): pl.pallas_call(functools.partial(kernel, sections, spans, across), out_sh...  77.1 us

commit v1 on v0

v1 whole, which is shorter than its diff:
```python
import functools
import math

import jax
import jax.numpy as jnp
from jax import lax
from jax.experimental import pallas as pl
from jax.experimental.pallas import tpu as pltpu
from jax.sharding import PartitionSpec as P

HEAD_SIZE = 128
COLUMNS = 256
PARTS = 4
AHEAD = 2
MOVED = (1, 3)
EXTRA = 16
VMEM_LIMIT = 50 * 1024 * 1024
MESH = pl.DeviceIdType.MESH


def kernel(sections, spans, across, q_ref, k_ref, v_ref, w_ref, o_ref, held, weight, stacked, acc, top,
           attended, projected, pair_send, pair_recv, far_send, pass_send, relay_send, span_recv, weight_sem, out_send, out_recv,
           own_sem, query_sem, aside, aside_recv, cross_send):
    rows, kv_width = k_ref.shape
    q_width = q_ref.shape[1]
    heads = kv_width // HEAD_SIZE
    group = q_width // kv_width
    chips = spans // 2
    pieces = weight.shape[0]
    section = lax.axis_index("pipe")
    me = lax.axis_index("ctx")
    chip, core = me // 2, lax.rem(me, 2)
    line, column = chip // across, lax.rem(chip, across)
    lines = chips // across
    following = lax.rem(section + 1, sections)
    before = lax.rem(section + sections - 1, sections)
    factor = math.log2(math.e) / math.sqrt(HEAD_SIZE)

    barrier = pltpu.get_barrier_semaphore()

    @pl.loop(1, spans)
    def _(step):
        pl.semaphore_signal(barrier, inc=1, device_id={"ctx": lax.rem(me + step, spans)}, device_id_type=MESH)

    @pl.loop(0, chips)
    def _(other):
        pl.semaphore_signal(
            barrier, inc=1, device_id={"pipe": before, "ctx": other * 2 + core}, device_id_type=MESH)

    def weight_copy(piece):
        return pltpu.make_async_copy(
            w_ref.at[:, pl.ds(pl.multiple_of(piece * COLUMNS, COLUMNS), COLUMNS)],
            weight.at[piece], weight_sem.at[piece])

    part_width = kv_width // PARTS

    def place(owner, side, which, part):
        return held.at[owner, which, part, pl.ds(pl.multiple_of(side * rows, rows), rows), :]

    def own_copy(which, part):
        return pltpu.make_async_copy(
            (k_ref, v_ref)[which].at[:, part * part_width:(part + 1) * part_width],
            place(chip, core, which, part), own_sem.at[which, part])

    def each_part(act):
        for part in range(PARTS):
            for which in range(2):
                act(which, part)

    def query_copy(head, member):
        at = head * group + member
        return pltpu.make_async_copy(
            q_ref.at[:, at * HEAD_SIZE:(at + 1) * HEAD_SIZE],
            stacked.at[head, member * rows:(member + 1) * rows, :], query_sem.at[at])

    each_part(lambda *at: own_copy(*at).start())
    for head in range(heads):
        for member in range(group):
            query_copy(head, member).start()

    @pl.loop(0, pieces)
    def _(piece):
        weight_copy(piece).start()

    each_part(lambda *at: own_copy(*at).wait())

    def pair_copy(which, part):
        return pltpu.make_async_remote_copy(
            place(chip, core, which, part), place(chip, core, which, part), pair_send.at[which, part],
            pair_recv.at[which, part], device_id={"ctx": chip * 2 + 1 - core}, device_id_type=MESH)

    def far_copy(target, which, part):
        return pltpu.make_async_remote_copy(
            place(chip, core, which, part), place(chip, core, which, part), far_send.at[target, which, part],
            span_recv.at[chip, core, which, part], device_id={"ctx": target * 2 + core}, device_id_type=MESH)

    def pass_copy(owner, which, part):
        return pltpu.make_async_remote_copy(
            place(owner, core, which, part), place(owner, core, which, part), pass_send.at[owner, which, part],
            span_recv.at[owner, core, which, part], device_id={"ctx": chip * 2 + 1 - core}, device_id_type=MESH)

    def relay_copy(owner, target, at, which, part):
        return pltpu.make_async_remote_copy(
            place(owner, core, which, part), place(owner, core, which, part), relay_send.at[owner, at, which, part],
            span_recv.at[owner, core, which, part], device_id={"ctx": target * 2 + core}, device_id_type=MESH)

    def each_own(part, act):
        @pl.loop(column + 1, across)
        def _(other):
            act(line * across + other, 0, part)
            act(line * across + other, 1, part)

        @pl.loop(line + 1, lines)
        def _(other):
            act(other * across + column, 1, part)
            act(other * across + column, 0, part)

    def each_relay(owner, which, part, act):
        beside = owner // across == line
        above = jnp.logical_not(beside) & (lax.rem(owner, across) == column)
        if which == 0:
            @pl.when(beside)
            def _():
                @pl.loop(line + 1, lines)
                def _(other):
                    act(owner, other * across + column, other, which, part)

            @pl.when(above)
            def _():
                @pl.loop(0, column)
                def _(other):
                    act(owner, line * across + other, other, which, part)
        else:
            @pl.when(above)
            def _():
                @pl.loop(1, across)
                def _(step):
                    other = lax.rem(column + step, across)
                    act(owner, line * across + other, other, which, part)

    def wait_span(owner, side, which, part):
        pltpu.make_async_remote_copy(
            place(owner, side, which, part), place(owner, side, which, part), pass_send.at[owner, which, part],
            span_recv.at[owner, side, which, part], device_id={"ctx": chip * 2 + 1 - core},
            device_id_type=MESH).wait_recv()

    pl.semaphore_wait(barrier, spans - 1 + chips)
    each_part(lambda *at: pair_copy(*at).start())

    for part in range(PARTS):
        each_own(part, lambda *at: far_copy(*at).start())

    for head in range(heads):
        for member in range(group):
            query_copy(head, member).wait()

    def block(owner, part, within, first):
        head = part * (heads // PARTS) + within
        lanes = slice(within * HEAD_SIZE, (within + 1) * HEAD_SIZE)
        scores = lax.dot_general(
            held[owner, 0, part, :, lanes], stacked[head], (((1,), (1,)), ((), ())),
            preferred_element_type=jnp.float32)
        if first:
            key = lax.broadcasted_iota(jnp.int32, scores.shape, 0)
            row = lax.rem(lax.broadcasted_iota(jnp.int32, scores.shape, 1), rows) + core * rows
            scores = jnp.where(key <= row, scores, -1e30)
        highest = jnp.max(scores, axis=0, keepdims=True)
        if not first:
            previous = top[head]
            highest = jnp.maximum(previous, highest)
            rescale = jnp.exp2((previous - highest) * factor)
        top[head] = highest
        weights = jnp.exp2((scores - highest) * factor).astype(jnp.bfloat16)
        values = held[owner, 1, part, :, lanes].T
        values = jnp.concatenate([values, jnp.ones((EXTRA, values.shape[1]), values.dtype)], axis=0)
        summed = jnp.dot(values, weights, preferred_element_type=jnp.float32)
        if first:
            acc[head] = summed
        else:
            acc[head] = acc[head] * rescale + summed

    for part in range(PARTS):
        for which in range(2):
            pair_copy(which, part).wait_recv()
        for within in range(heads // PARTS):
            block(chip, part, within, True)

    near = line + column
    apart = line * (across - 1)

    def source(step):
        early = step < near * PARTS
        count = jnp.maximum(jnp.where(early, near, apart), 1)
        order = jnp.where(early, step, step - near * PARTS)
        part = order // count
        nth = order - part * count
        others = max(across - 1, 1)
        direct = jnp.where(
            nth < column, line * across + column - 1 - nth, (line - 1 - nth + column) * across + column)
        relayed = (line - 1 - nth // others) * across + lax.rem(column + 1 + lax.rem(nth, others), across)
        return jnp.where(early, direct, relayed), part

    @pl.loop(0, jnp.where(chip > 0, chip * PARTS + AHEAD, 0))
    def _(step):
        @pl.when(step < chip * PARTS)
        def _():
            owner, part = source(step)
            for which in range(2):
                wait_span(owner, core, which, part)
                each_relay(owner, which, part, lambda *at: relay_copy(*at).start())
                pass_copy(owner, which, part).start()

        @pl.when(step >= AHEAD)
        def _():
            owner, part = source(step - AHEAD)
            for which in range(2):
                wait_span(owner, 1 - core, which, part)
            for within in range(heads // PARTS):
                block(owner, part, within, False)

    for head in range(heads):
        for member in range(group):
            share = acc[head, :, member * rows:(member + 1) * rows]
            attended[:, (head * group + member) * HEAD_SIZE:(head * group + member + 1) * HEAD_SIZE] = (
                share[:HEAD_SIZE] / share[HEAD_SIZE:HEAD_SIZE + 1]).T.astype(jnp.bfloat16)

    def out_copy(piece):
        return pltpu.make_async_remote_copy(
            projected.at[piece],
            o_ref.at[:, pl.ds(pl.multiple_of(piece * COLUMNS, COLUMNS), COLUMNS)],
            out_send.at[piece], out_recv.at[piece], device_id={"pipe": following}, device_id_type=MESH)

    late = chips - chips // 2
    slot_of = lax.rem(chip + 2 * chips - late, 2)
    moved = jnp.where(chip >= late, jnp.where(slot_of == 0, MOVED[0], MOVED[1]), 0)

    def aside_copy(piece):
        return pltpu.make_async_remote_copy(
            projected.at[piece], aside.at[slot_of, piece], out_send.at[piece],
            aside_recv.at[slot_of, piece],
            device_id={"ctx": (chip - late) // 2 * 2 + core}, device_id_type=MESH)

    def cross_copy(slot, piece):
        return pltpu.make_async_remote_copy(
            aside.at[slot, piece],
            o_ref.at[:, pl.ds(pl.multiple_of(piece * COLUMNS, COLUMNS), COLUMNS)],
            cross_send.at[slot, piece], out_recv.at[piece],
            device_id={"pipe": following, "ctx": (late + chip * 2 + slot) * 2 + core}, device_id_type=MESH)

    def each_carried(act):
        for slot in range(2):
            @pl.when(late + chip * 2 + slot < chips)
            def _():
                @pl.loop(0, MOVED[slot])
                def _(piece):
                    act(slot, piece)

    def carry(slot, piece):
        pltpu.make_async_remote_copy(
            aside.at[slot, piece], aside.at[slot, piece], cross_send.at[slot, piece],
            aside_recv.at[slot, piece], device_id={"pipe": following}, device_id_type=MESH).wait_recv()
        cross_copy(slot, piece).start()

    @pl.loop(0, pieces)
    def _(piece):
        weight_copy(piece).wait()
        projected[piece] = jnp.dot(
            attended[...], weight[piece], preferred_element_type=jnp.float32).astype(jnp.bfloat16)

        @pl.when(piece < moved)
        def _():
            aside_copy(piece).start()

        @pl.when(piece >= moved)
        def _():
            out_copy(piece).start()

    each_carried(carry)

    each_part(lambda *at: pair_copy(*at).wait_send())

    for part in range(PARTS):
        each_own(part, lambda *at: far_copy(*at).wait_send())

    @pl.loop(0, chip)
    def _(owner):
        for part in range(PARTS):
            for which in range(2):
                each_relay(owner, which, part, lambda *at: relay_copy(*at).wait_send())
                pass_copy(owner, which, part).wait_send()

    each_carried(lambda *at: cross_copy(*at).wait_send())

    @pl.loop(0, pieces)
    def _(piece):
        out_copy(piece).wait()


def per_device(sections, spans, queries, keys, values, out_weight):
    rows, q_width = queries.shape[1:]
    kv_width = keys.shape[2]
    width = out_weight.shape[2]
    heads = kv_width // HEAD_SIZE
    stack = q_width // kv_width * rows
    pieces = width // COLUMNS
    chips = spans // 2
    across = math.isqrt(chips)
    across = across if chips % across == 0 else chips
    hbm = pl.BlockSpec(memory_space=pltpu.HBM)
    handed = pl.pallas_call(
        functools.partial(kernel, sections, spans, across),
        out_shape=jax.ShapeDtypeStruct((rows, width), jnp.bfloat16),
        in_specs=[hbm] * 4,
        out_specs=pl.BlockSpec(memory_space=pl.ANY),
        scratch_shapes=[
            pltpu.VMEM((chips, 2, PARTS, 2 * rows, kv_width // PARTS), jnp.bfloat16),
            pltpu.VMEM((pieces, q_width, COLUMNS), jnp.bfloat16),
            pltpu.VMEM((heads, stack, HEAD_SIZE), jnp.bfloat16),
            pltpu.VMEM((heads, HEAD_SIZE + EXTRA, stack), jnp.float32),
            pltpu.VMEM((heads, 1, stack), jnp.float32),
            pltpu.VMEM((rows, q_width), jnp.bfloat16),
            pltpu.VMEM((pieces, rows, COLUMNS), jnp.bfloat16),
            pltpu.SemaphoreType.DMA((2, PARTS)),
            pltpu.SemaphoreType.DMA((2, PARTS)),
            pltpu.SemaphoreType.DMA((chips, 2, PARTS)),
            pltpu.SemaphoreType.DMA((chips, 2, PARTS)),
            pltpu.SemaphoreType.DMA((chips, max(across, chips // across), 2, PARTS)),
            pltpu.SemaphoreType.DMA((chips, 2, 2, PARTS)),
            pltpu.SemaphoreType.DMA((pieces,)),
            pltpu.SemaphoreType.DMA((pieces,)),
            pltpu.SemaphoreType.DMA((pieces,)),
            pltpu.SemaphoreType.DMA((2, PARTS)),
            pltpu.SemaphoreType.DMA((q_width // HEAD_SIZE,)),
            pltpu.VMEM((2, max(MOVED), rows, COLUMNS), jnp.bfloat16),
            pltpu.SemaphoreType.DMA((2, max(MOVED))),
            pltpu.SemaphoreType.DMA((2, max(MOVED))),
        ],
        compiler_params=pltpu.CompilerParams(
            collective_id=0, has_side_effects=True, vmem_limit_bytes=VMEM_LIMIT),
    )(*(pltpu.with_memory_space_constraint(each[0], pltpu.HBM) for each in (queries, keys, values, out_weight)))
    return handed[None]


def solution(mesh):
    placed = (
        P("pipe", "ctx", None),
        P("pipe", "ctx", None),
        P("pipe", "ctx", None),
        P("pipe", None, None),
    )
    return jax.shard_map(
        functools.partial(per_device, mesh.shape["pipe"], mesh.shape["ctx"]),
        mesh=mesh, in_specs=placed, out_specs=P("pipe", "ctx", None), check_vma=False
    )
```

time: 78.6 us -> 74.8 us (0.952)
  Pallas kernels: 77.1 us -> 73.3 us
    pallas_call x1, Pallas kernels: 77.1 us -> 73.3 us  [per_device(): pl.pallas_call(functools.partial(kernel, sections, spans, across), out_sh...]
where the time goes in v1:
time: 74.8 us; the launch traced here: 74.6 us
  Pallas kernels  73.3 us (98%)
  local copies, waits for them, and re-layouts  1.32 us (2%)
    pallas_call x1, Pallas kernels, per_device(): pl.pallas_call(functools.partial(kernel, sections, spans, across), out_sh...  73.3 us

profile of v1, /device:TPU:4, one launch (start us, length us, event | category | flops | bytes accessed | tf_op | source)
XLA Modules:
  0.0 74.6 jit_solution(13835017355916295629)
XLA Ops:
  0.0 73.3 %shard_map.46 = bf16[256,4096]{1,0:T(8,128)(2,1)S(1)} custom-call(bf16[256,2048]{1,0:T(8,128)(2,1)} %bitcast.7, bf16[256,512]{1,0:T(8,128)(2,1)} %bitcast.8, bf16[256,512]{1,0:T(8,128)(2,1)} %bitcast.9, bf16[2048,4096]{1,0:T(8,128)(2,1)} %bitcast.6), custom_call_target="tpu_custom_call" | custom-call | tf_op jit(solution)/shard_map/pallas_call | solution.py:310
  73.3 1.3 %copy.6 = bf16[1,256,4096]{2,1,0:T(8,128)(2,1)} copy(bf16[1,256,4096]{2,1,0:T(8,128)(2,1)S(1)} %bitcast.5) | data formatting | bytes 4194304
